TPU v7x, 32 devices: a whole 2x2x4 slice. The times are simulated.
32 devices in a mesh: row: 4 (over y, x), col: 4 (over z), cores: 2 (over core).
Axes of the slice: x: 2, y: 2, z: 4, core: 2. Of those that a mesh axis runs over, the one named last changes fastest.
Arguments:
- multipoles: bfloat16 [315, 2048], P(None, ('col', 'row')), may hold values from -6 to 6
- operators: bfloat16 [40, 315, 315], P('cores'), may hold values from -0.0078125 to 0.0078125
- classes: int32 [2048, 2048], P('row', 'col'), may hold values from 0 to 39, as said below
- separated: int32 [4, 4], P('row', 'col'), may hold values 0 or 1
- owners: int32 [2048], P('row'), may hold values from 0 to 7, as said below
Outputs:
- owned: float32 [315, 4096], P(None, ('row', 'col', 'cores'))
Inputs may be any that keep to these rules, and one draw needn't show every extreme that they name: `owners`: in each block of 512 cells (cells b * 512 to b * 512 + 511) no owner holds more than 128 cells, and in every block one owner holds exactly 128. Cell t sits at (t % 8, (t // 8) % 4, t // 32) on a periodic grid of 8 x 4 x 2048 // 32 cells; classes[t, s] depends only on the wrapped offset between the positions of t and s.
All inputs are finite; a program needn't handle non-finite values. No bound on the sum of `separated` on one device may be relied on, other than what follows from the above.
Results may differ from a plain program's by a relative error of at most 0.0029.
Values may be sent and summed in bfloat16 or wider, within the bound.
A program may use at most 64 MiB of HBM per device.

v0:
```python
import jax
import jax.numpy as jnp
from jax import lax
from jax.sharding import PartitionSpec as P


def shards(multipoles, operators, classes, separated, owners):
    count = operators.shape[0]
    targets, sources = classes.shape
    base = lax.axis_index("cores") * count
    moved = jnp.einsum(
        "kqp,ps->kqs",
        operators,
        lax.all_gather(multipoles, "row", axis=1, tiled=True),
        preferred_element_type=jnp.float32,
    ).astype(jnp.bfloat16)
    spread = separated.shape[1]
    wide_mask = jnp.repeat(separated[0], sources // spread)
    labels = jnp.arange(count, dtype=jnp.int32) + base
    pick = (
        (classes[None, :, :] == labels[:, None, None]) & (wide_mask[None, None, :] == 1)
    ).astype(jnp.bfloat16)
    partial_value = jnp.einsum("kts,kqs->qt", pick, moved, preferred_element_type=jnp.float32)
    group = lax.axis_size(("col", "cores"))
    slots = 2 * targets // group
    member = lax.axis_index(("col", "cores"))
    hit = (owners[None, :] == jnp.arange(group, dtype=jnp.int32)[:, None]).astype(jnp.int32)
    before = jnp.cumsum(hit, axis=1) - hit
    rank = jnp.sum(before * hit, axis=0)
    slot_ids = jnp.arange(slots, dtype=jnp.int32)
    share = lax.psum_scatter(partial_value, ("col", "cores"), scatter_dimension=1, tiled=True)
    width = share.shape[1]
    share_owner = lax.dynamic_slice_in_dim(owners, member * width, width)
    outgoing = jnp.where(
        share_owner[None, None, :] == jnp.arange(group, dtype=jnp.int32)[:, None, None],
        share[None, :, :],
        0.0,
    )
    incoming = lax.all_to_all(outgoing, ("col", "cores"), split_axis=0, concat_axis=0, tiled=True)
    place = ((owners[None, :] == member) & (rank[None, :] == slot_ids[:, None])).astype(jnp.float32)
    owned = jnp.einsum(
        "spj,csj->pc", incoming, place.reshape(slots, group, width), precision=lax.Precision.HIGHEST
    )
    return owned


def solution(mesh):
    return jax.shard_map(
        shards,
        mesh=mesh,
        in_specs=(
            P(None, ("col", "row")),
            P("cores", None, None),
            P("row", "col"),
            P("row", "col"),
            P("row"),
        ),
        out_specs=P(None, ("row", "col", "cores")),
        check_vma=False,
    )
```

profile of v0, /device:TPU:0, one launch (start us, length us, event | category | flops | bytes accessed | tf_op | source)
XLA Modules:
  0.0 97.6 jit_solution(1368173200117882711)
XLA Ops:
  6.5 0.0 reduce-scatter.2.cloned.1.call-start
  6.5 11.0 %all_gather.3 = bf16[315,512]{1,0:T(8,128)(2,1)S(1)} all-gather(bf16[315,128]{1,0:T(8,128)(2,1)} %param.5), channel_id=1, replica_groups=mesh['row'=4,'col'=4,'cores'=2] {'row'}, dimensions={1}, use_global_device_ids=true | all-gather | bytes 403200 | tf_op jit(solution)/shard_map/all_gather | solution.py:14
  18.2 0.0 copy-start
  18.2 12.6 %fusion.6 = f32[315,512]{0,1:T(8,128)} fusion(s32[512,512]{1,0:T(8,128)} %param.7, s32[20]{0:T(128)S(1)} %iota_add_fusion, pred[]{:T(512)} %bitcast.1, bf16[20,315,315]{2,1,0:T(8,128)(2,1)} %param.6, bf16[315,512]{1,0:T(8,128)(2,1)S(1)} %all_gather.3), kind=kOutput, calls=%fused_computation.7 | convolution fusion | flops 5348853760 | bytes 5985337 | tf_op jit(solution)/shard_map/kts,kqs->qt/dot_general | solution.py:23
  30.8 0.0 reduce-scatter.2.cloned.1.call-update
  30.8 0.0 copy-done
  30.8 0.1 dynamic_slice.3
  30.9 31.8 %reduce-scatter.2.cloned.1.call-done = f32[315,64]{0,1:T(8,128)} async-done(((f32[315,512]{0,1:T(8,128)}), f32[315,64]{0,1:T(8,128)}) %reduce-scatter.2.cloned.1.call-update) | async-done | bytes 80656 | tf_op jit(solution)/shard_map/reduce_scatter | solution.py:31
  62.7 1.9 %broadcast_select_fusion = f32[8,315,64]{1,2,0:T(8,128)} fusion(f32[315,64]{0,1:T(8,128)} %reduce-scatter.2.cloned.1.call-done, pred[8,64]{1,0:T(8,128)(4,1)S(1)} %iota_compare_fusion.2), kind=kLoop, calls=%fused_computation.9 | loop fusion | flops 161280 | bytes 726272 | tf_op jit(solution)/shard_map/jit(_where)/select_n | solution.py:34
  64.7 3.5 %all-to-all-start = ((f32[8,315,64]{1,2,0:T(8,128)}), f32[8,315,64]{1,2,0:T(8,128)S(1)}, u32[]{:S(2)}, u32[]{:S(2)}) async-start(f32[8,315,64]{1,2,0:T(8,128)} %broadcast_select_fusion), calls=%async_computation.1 | async-start | bytes 1572864 | tf_op jit(solution)/shard_map/all_to_all | solution.py:39
  68.2 1.1 %reduce-window.6 = s32[8,4,128]{2,0,1:T(8,128)S(1)} reduce-window(s32[8,4,128]{2,0,1:T(8,128)S(1)} %fusion.15, s32[]{:T(128)} %constant.22.clone.1), window={size=1x1x128 pad=0_0x0_0x127_0}, to_apply=%region_1.2 | reduce-window | flops 520192 | bytes 32772 | tf_op jit(solution)/shard_map/reduce-window
  69.4 0.2 slice_reduce_fusion
  69.6 0.1 select_reduce_fusion
  69.7 0.1 eq.93
  69.8 0.1 and.23
  69.9 19.2 %all-to-all-done = f32[8,315,64]{1,2,0:T(8,128)S(1)} async-done(((f32[8,315,64]{1,2,0:T(8,128)}), f32[8,315,64]{1,2,0:T(8,128)S(1)}, u32[]{:S(2)}, u32[]{:S(2)}) %all-to-all-start) | async-done | bytes 645152 | tf_op jit(solution)/shard_map/all_to_all | solution.py:39
  89.1 1.6 %convolution_bitcast_fusion = f32[315,128]{1,0:T(8,128)} fusion(f32[8,315,64]{1,2,0:T(8,128)S(1)} %all-to-all-done, s32[8,64]{1,0:T(8,128)S(1)} %eq.93, pred[8,64]{1,0:T(8,128)(4,1)S(1)} %and.23), kind=kOutput, calls=%fused_computation.8 | convolution fusion | flops 247857152 | bytes 808960 | tf_op jit(solution)/shard_map/spj,csj->pc/dot_general | solution.py:41
  (6 shorter events, 0.1 us)
Async XLA Ops:
  6.5 56.2 %reduce-scatter.2.cloned.1.call-start = ((), (), s32[]{:S(2)}) async-start(), calls=%async_computation.2 | async-start | bytes 884736 | tf_op jit(solution)/shard_map/reduce_scatter | solution.py:31
  18.2 12.6 %copy-start = (s32[512]{0:T(512)S(1)}, s32[512]{0:T(512)}, u32[]{:S(2)}) copy-start(s32[512]{0:T(512)} %param.9) | copy-start | bytes 6148
  64.7 24.4 %all-to-all-start = ((f32[8,315,64]{1,2,0:T(8,128)}), f32[8,315,64]{1,2,0:T(8,128)S(1)}, u32[]{:S(2)}, u32[]{:S(2)}) async-start(f32[8,315,64]{1,2,0:T(8,128)} %broadcast_select_fusion), calls=%async_computation.1 | async-start | bytes 1572864 | tf_op jit(solution)/shard_map/all_to_all | solution.py:39
Sparse Core Ops, SparseCore 0:
  30.9 31.7 reduce-scatter.1
where the time goes:
time: 97.8 us; the launch traced here: 97.6 us
  waiting for transfers between devices  51.1 us (52%)
  matrix products  14.2 us (15%)
  between operations  14.1 us (14%)
  blocking collectives  11 us (11%)
  starting transfers between devices  3.55 us (4%)
  other arithmetic  3.2 us (3%)
    reduce_scatter x1, waiting for transfers between devices, shards(): lax.psum_scatter(partial_value, ('col', 'cores'), scatter_dimension=1, ti...  31.8 us
    all_to_all x1, waiting for transfers between devices, shards(): lax.all_to_all(outgoing, ('col', 'cores'), split_axis=0, concat_axis=0, t...  19.2 us
    dot_general x1, matrix products, shards(): jnp.einsum('kts,kqs->qt', pick, moved, preferred_element_type=jnp.float32)  12.6 us
    all_gather x1, blocking collectives, shards(): lax.all_gather(multipoles, 'row', axis=1, tiled=True)  11 us
    all_to_all x1, starting transfers between devices, shards(): lax.all_to_all(outgoing, ('col', 'cores'), split_axis=0, concat_axis=0, t...  3.55 us
  transfers between devices with their start and end apart: 2, of which 2 were waited for; matrix products, arithmetic and copies ran while one was open for 2% of the time, Pallas kernels for 0%

commit v1 on v0

--- a/solution.py
+++ b/solution.py
@@ -2,6 +2,19 @@
 import jax.numpy as jnp
 from jax import lax
 from jax.sharding import PartitionSpec as P
+
+
+def collect(array, axis, dim):
+    ways = lax.axis_size(axis)
+    up = [(d, (d + 1) % ways) for d in range(ways)]
+    down = [(d, (d - 1) % ways) for d in range(ways)]
+    earlier, later = ([array], [array])
+    for _ in range(ways // 2):
+        earlier.append(lax.ppermute(earlier[-1], axis, up))
+    for _ in range((ways - 1) // 2):
+        later.append(lax.ppermute(later[-1], axis, down))
+    line = jnp.concatenate([*earlier[::-1], *later[1:]], axis=dim)
+    return jnp.roll(line, (lax.axis_index(axis) - ways // 2) * array.shape[dim], axis=dim)
 
 
 def shards(multipoles, operators, classes, separated, owners):
@@ -9,10 +22,7 @@
     targets, sources = classes.shape
     base = lax.axis_index("cores") * count
     moved = jnp.einsum(
-        "kqp,ps->kqs",
-        operators,
-        lax.all_gather(multipoles, "row", axis=1, tiled=True),
-        preferred_element_type=jnp.float32,
+        "kqp,ps->kqs", operators, collect(multipoles, "row", 1), preferred_element_type=jnp.float32
     ).astype(jnp.bfloat16)
     spread = separated.shape[1]
     wide_mask = jnp.repeat(separated[0], sources // spread)

time: 97.8 us -> 101 us (1.033)
  blocking collectives: 11 us -> 0 us
  waiting for transfers between devices: 51.1 us -> 58.1 us
  starting transfers between devices: 3.55 us -> 8.85 us
  local copies, waits for them, and re-layouts: 0.47 us -> 2.42 us
    all_gather x1 -> x0, blocking collectives: 11 us -> none  [shards(): lax.all_gather(multipoles, 'row', axis=1, tiled=True)]
    ppermute x0 -> x3, waiting for transfers between devices: none -> 6.27 us  [the longest x2 6.27 us: collect(): earlier.append(lax.ppermute(earlier[-1], axis, up))]
    ppermute x0 -> x3, starting transfers between devices: none -> 5.3 us  [the longest x2 4.34 us: collect(): earlier.append(lax.ppermute(earlier[-1], axis, up))]
    unnamed x2 -> x9, local copies, waits for them, and re-layouts: 0.01 us -> 1.94 us
  transfers between devices with their start and end apart: 2 -> 5, of which waited for: 2 -> 4; matrix products, arithmetic and copies ran while one was open for 2% -> 3% of each run, Pallas kernels for 0% -> 0%
where the time goes in v1:
time: 101 us
  waiting for transfers between devices  58.1 us (58%)
  matrix products  14.2 us (14%)
  between operations  14.2 us (14%)
  starting transfers between devices  8.85 us (9%)
  other arithmetic  3.19 us (3%)
  local copies, waits for them, and re-layouts  2.42 us (2%)
    reduce_scatter x1, waiting for transfers between devices, shards(): lax.psum_scatter(partial_value, ('col', 'cores'), scatter_dimension=1, ti...  32.6 us
    all_to_all x1, waiting for transfers between devices, shards(): lax.all_to_all(outgoing, ('col', 'cores'), split_axis=0, concat_axis=0, t...  19.2 us
    dot_general x1, matrix products, shards(): jnp.einsum('kts,kqs->qt', pick, moved, preferred_element_type=jnp.float32)  12.6 us
    ppermute x2, waiting for transfers between devices, collect(): earlier.append(lax.ppermute(earlier[-1], axis, up))  6.27 us
    ppermute x2, starting transfers between devices, collect(): earlier.append(lax.ppermute(earlier[-1], axis, up))  4.34 us
    all_to_all x1, starting transfers between devices, shards(): lax.all_to_all(outgoing, ('col', 'cores'), split_axis=0, concat_axis=0, t...  3.55 us
  transfers between devices with their start and end apart: 5, of which 4 were waited for; matrix products, arithmetic and copies ran while one was open for 3% of the time, Pallas kernels for 0%

profile of v1, /device:TPU:0, one launch (start us, length us, event | category | flops | bytes accessed | tf_op | source)
XLA Modules:
  0.0 100.9 jit_solution(10613317040405938562)
XLA Ops:
  6.5 0.0 reduce-scatter.2.cloned.1.call-start
  6.5 2.9 %collective-permute-start = (bf16[315,128]{1,0:T(8,128)(2,1)}, bf16[315,128]{1,0:T(8,128)(2,1)S(1)}, u32[]{:S(2)}, u32[]{:S(2)}) collective-permute-start(bf16[315,128]{1,0:T(8,128)(2,1)} %param.5), channel_id=1, source_target_pairs={{0,8},{8,16},{16,24},{24,0},{1,9},{9,17},{17,25},{25,1},{2,10},{10... | collective-permute-start | bytes 241928 | tf_op jit(solution)/shard_map/ppermute | solution.py:13
  9.5 1.0 collective-permute-start.2
  11.1 2.3 %collective-permute-done = bf16[315,128]{1,0:T(8,128)(2,1)S(1)} collective-permute-done((bf16[315,128]{1,0:T(8,128)(2,1)}, bf16[315,128]{1,0:T(8,128)(2,1)S(1)}, u32[]{:S(2)}, u32[]{:S(2)}) %collective-permute-start) | collective-permute-done | bytes 80672 | tf_op jit(solution)/shard_map/ppermute | solution.py:13
  13.4 1.4 %collective-permute-start.1 = (bf16[315,128]{1,0:T(8,128)(2,1)S(1)}, bf16[315,128]{1,0:T(8,128)(2,1)S(1)}, u32[]{:S(2)}, u32[]{:S(2)}) collective-permute-start(bf16[315,128]{1,0:T(8,128)(2,1)S(1)} %collective-permute-done), channel_id=1, source_target_pairs={{0,8},{8,16},{16,24},{24,0},{1,9},{9,17},{17,25},{25,1},{2,10},{10... | collective-permute-start | bytes 241928 | tf_op jit(solution)/shard_map/ppermute | solution.py:13
  14.8 3.9 %collective-permute-done.1 = bf16[315,128]{1,0:T(8,128)(2,1)S(1)} collective-permute-done((bf16[315,128]{1,0:T(8,128)(2,1)S(1)}, bf16[315,128]{1,0:T(8,128)(2,1)S(1)}, u32[]{:S(2)}, u32[]{:S(2)}) %collective-permute-start.1) | collective-permute-done | bytes 80672 | tf_op jit(solution)/shard_map/ppermute | solution.py:13
  18.8 0.9 constant_dynamic-update-slice_fusion.5
  19.7 0.0 collective-permute-done.2
  19.8 0.9 constant_dynamic-update-slice_fusion.1
  20.8 0.0 copy-start
  20.8 12.6 %fusion.7 = f32[315,512]{0,1:T(8,128)} fusion(s32[512,512]{1,0:T(8,128)} %param.7, s32[20]{0:T(128)S(1)} %iota_add_fusion, pred[]{:T(512)} %bitcast.2, bf16[20,315,315]{2,1,0:T(8,128)(2,1)} %param.6, bf16[315,1024]{1,0:T(8,128)(2,1)S(1)} %constant_dynamic-update-slice_fusion, s32[]{:T(128)S(6)} %select_n.22), kind=kOutput, calls=%fused_computation.8 | convolution fusion | flops 5348853760 | bytes 5990893 | tf_op jit(solution)/shard_map/kts,kqs->qt/dot_general | solution.py:33
  33.4 0.0 reduce-scatter.2.cloned.1.call-update
  33.4 0.0 copy-done
  33.4 0.1 dynamic_slice.7
  33.5 32.6 %reduce-scatter.2.cloned.1.call-done = f32[315,64]{0,1:T(8,128)} async-done(((f32[315,512]{0,1:T(8,128)}), f32[315,64]{0,1:T(8,128)}) %reduce-scatter.2.cloned.1.call-update) | async-done | bytes 80656 | tf_op jit(solution)/shard_map/reduce_scatter | solution.py:41
  66.1 1.9 %broadcast_select_fusion = f32[8,315,64]{1,2,0:T(8,128)} fusion(f32[315,64]{0,1:T(8,128)} %reduce-scatter.2.cloned.1.call-done, pred[8,64]{1,0:T(8,128)(4,1)S(1)} %iota_compare_fusion.2), kind=kLoop, calls=%fused_computation.10 | loop fusion | flops 161280 | bytes 726272 | tf_op jit(solution)/shard_map/jit(_where)/select_n | solution.py:44
  68.0 3.5 %all-to-all-start = ((f32[8,315,64]{1,2,0:T(8,128)}), f32[8,315,64]{1,2,0:T(8,128)S(1)}, u32[]{:S(2)}, u32[]{:S(2)}) async-start(f32[8,315,64]{1,2,0:T(8,128)} %broadcast_select_fusion), calls=%async_computation.1 | async-start | bytes 1572864 | tf_op jit(solution)/shard_map/all_to_all | solution.py:49
  71.6 0.1 and.31
  71.7 1.1 %reduce-window.6 = s32[8,4,128]{2,0,1:T(8,128)S(1)} reduce-window(s32[8,4,128]{2,0,1:T(8,128)S(1)} %fusion.20, s32[]{:T(128)} %constant.45.clone.1), window={size=1x1x128 pad=0_0x0_0x127_0}, to_apply=%region_1.2 | reduce-window | flops 520192 | bytes 32772 | tf_op jit(solution)/shard_map/reduce-window
  72.8 0.2 slice_reduce_fusion
  73.1 0.1 select_reduce_fusion
  73.1 0.1 eq.96
  73.2 19.2 %all-to-all-done = f32[8,315,64]{1,2,0:T(8,128)S(1)} async-done(((f32[8,315,64]{1,2,0:T(8,128)}), f32[8,315,64]{1,2,0:T(8,128)S(1)}, u32[]{:S(2)}, u32[]{:S(2)}) %all-to-all-start) | async-done | bytes 645152 | tf_op jit(solution)/shard_map/all_to_all | solution.py:49
  92.5 1.6 %convolution_bitcast_fusion = f32[315,128]{1,0:T(8,128)} fusion(f32[8,315,64]{1,2,0:T(8,128)S(1)} %all-to-all-done, s32[8,64]{1,0:T(8,128)S(1)} %eq.96, pred[8,64]{1,0:T(8,128)(4,1)S(1)} %and.31), kind=kOutput, calls=%fused_computation.9 | convolution fusion | flops 247857152 | bytes 808960 | tf_op jit(solution)/shard_map/spj,csj->pc/dot_general | solution.py:51
  (12 shorter events, 0.2 us)
Async XLA Ops:
  6.5 59.6 %reduce-scatter.2.cloned.1.call-start = ((), (), s32[]{:S(2)}) async-start(), calls=%async_computation.2 | async-start | bytes 884736 | tf_op jit(solution)/shard_map/reduce_scatter | solution.py:41
  6.5 6.9 %collective-permute-start = (bf16[315,128]{1,0:T(8,128)(2,1)}, bf16[315,128]{1,0:T(8,128)(2,1)S(1)}, u32[]{:S(2)}, u32[]{:S(2)}) collective-permute-start(bf16[315,128]{1,0:T(8,128)(2,1)} %param.5), channel_id=1, source_target_pairs={{0,8},{8,16},{16,24},{24,0},{1,9},{9,17},{17,25},{25,1},{2,10},{10... | collective-permute-start | bytes 241928 | tf_op jit(solution)/shard_map/ppermute | solution.py:13
  9.5 10.3 %collective-permute-start.2 = (bf16[315,128]{1,0:T(8,128)(2,1)}, bf16[315,128]{1,0:T(8,128)(2,1)S(1)}, u32[]{:S(2)}, u32[]{:S(2)}) collective-permute-start(bf16[315,128]{1,0:T(8,128)(2,1)} %param.5), channel_id=1, source_target_pairs={{0,24},{8,0},{16,8},{24,16},{1,25},{9,1},{17,9},{25,17},{2,26},{10... | collective-permute-start | bytes 241928 | tf_op jit(solution)/shard_map/ppermute | solution.py:15
  13.4 5.3 %collective-permute-start.1 = (bf16[315,128]{1,0:T(8,128)(2,1)S(1)}, bf16[315,128]{1,0:T(8,128)(2,1)S(1)}, u32[]{:S(2)}, u32[]{:S(2)}) collective-permute-start(bf16[315,128]{1,0:T(8,128)(2,1)S(1)} %collective-permute-done), channel_id=1, source_target_pairs={{0,8},{8,16},{16,24},{24,0},{1,9},{9,17},{17,25},{25,1},{2,10},{10... | collective-permute-start | bytes 241928 | tf_op jit(solution)/shard_map/ppermute | solution.py:13
  20.8 12.6 %copy-start = (s32[512]{0:T(512)S(1)}, s32[512]{0:T(512)}, u32[]{:S(2)}) copy-start(s32[512]{0:T(512)} %param.9) | copy-start | bytes 6148
  68.0 24.4 %all-to-all-start = ((f32[8,315,64]{1,2,0:T(8,128)}), f32[8,315,64]{1,2,0:T(8,128)S(1)}, u32[]{:S(2)}, u32[]{:S(2)}) async-start(f32[8,315,64]{1,2,0:T(8,128)} %broadcast_select_fusion), calls=%async_computation.1 | async-start | bytes 1572864 | tf_op jit(solution)/shard_map/all_to_all | solution.py:49
Sparse Core Ops, SparseCore 0:
  33.5 32.5 reduce-scatter.1
